TPU v7x, 128 devices: a whole 4x4x4 slice. The times are simulated.
128 devices in a mesh: cell: 16 (over x, z_hi, core), tm: 8 (over y, z_lo).
Axes of the slice: x: 4, y: 4, z: 4 (z_hi: 2, z_lo: 2; z = z_hi * 2 + z_lo), core: 2. Of those that a mesh axis runs over, the one named last changes fastest.
Arguments:
- window: float32 [16384, 16384], P('cell', 'tm'), may hold values from -0.09375 to 0.09375
- range_test: float32 [16384, 256], P('tm'), may hold values from -0.046875 to 0.046875
- co_test: float32 [256, 16384], P(None, 'cell'), may hold values from -0.046875 to 0.046875
- core_left: float32 [512, 16384], P(None, 'cell'), may hold values from -0.046875 to 0.046875
- core_right: float32 [512, 16384], P(None, 'tm'), may hold values from -0.046875 to 0.046875
Outputs:
- range_basis: float32 [16384, 256], P('cell')
- co_basis: float32 [256, 16384], P(None, 'tm')
- core: float32 [256, 256], replicated
All inputs are finite; a program needn't handle non-finite values.
Results may differ from a plain program's by a relative error of at most 0.00023.
Values sent between devices are 32-bit elements; how exact they have to be, the bound alone decides.
A program may use at most 128 MiB of HBM per device.

v0:
```python
import math
import jax
import jax.numpy as jnp
from jax import lax
from jax.sharding import PartitionSpec as P


def inner_rows(left, right):
    return lax.dot_general(left, right, (((0,), (0,)), ((), ())), precision=lax.Precision.HIGHEST)


def inner_cols(left, right):
    return lax.dot_general(left, right, (((1,), (1,)), ((), ())), precision=lax.Precision.HIGHEST)


def product(left, right):
    return jnp.dot(left, right, precision=lax.Precision.HIGHEST, preferred_element_type=jnp.float32)


def per_device(window, range_test, co_test, core_left, core_right):
    rows_total = window.shape[0] * lax.axis_size("cell")
    cols_total = window.shape[1] * lax.axis_size("tm")
    range_term = product(window, range_test)
    co_term = product(co_test, window)
    left_window = product(core_left, window)
    core_term = inner_cols(left_window, core_right)
    sketch_z = lax.psum(core_term, ("cell", "tm"))
    range_full = lax.psum(range_term, "tm")
    co_full = lax.psum(co_term, "cell")
    gram_y = lax.psum(inner_rows(range_full, range_full) / rows_total, "cell")
    gram_w = lax.psum(inner_cols(co_full, co_full) / cols_total, "tm")
    lower_y = jnp.linalg.cholesky(gram_y)
    lower_w = jnp.linalg.cholesky(gram_w)
    range_basis = jax.scipy.linalg.solve_triangular(lower_y, range_full.T, lower=True).T
    co_basis = jax.scipy.linalg.solve_triangular(lower_w, co_full, lower=True)
    left_image = lax.psum(product(core_left, range_basis), "cell")
    right_image = lax.psum(inner_cols(core_right, co_basis), "tm")
    gram_left = inner_rows(left_image, left_image)
    gram_right = inner_rows(right_image, right_image)
    projected = inner_rows(left_image, sketch_z)
    left_solved = jax.scipy.linalg.cho_solve((jnp.linalg.cholesky(gram_left), True), projected)
    middle = product(left_solved, right_image)
    core = jax.scipy.linalg.cho_solve((jnp.linalg.cholesky(gram_right), True), middle.T).T
    core = core * math.sqrt(rows_total * cols_total)
    return (range_basis, co_basis, core)


def solution(mesh):
    return jax.shard_map(
        per_device,
        mesh=mesh,
        in_specs=(P("cell", "tm"), P("tm", None), P(None, "cell"), P(None, "cell"), P(None, "tm")),
        out_specs=(P("cell", None), P(None, "tm"), P()),
        check_vma=False,
    )
```

profile of v0, /device:TPU:0, one launch (start us, length us, event | category | flops | bytes accessed | tf_op | source)
XLA Modules:
  0.0 920.8 jit_solution(13198876106782574047)
XLA Ops:
  7.2 10.7 %fusion.50 = f32[1024,256]{1,0:T(8,128)} fusion(f32[1024,2048]{1,0:T(8,128)} %param.6, f32[2048,256]{1,0:T(8,128)} %param.7), kind=kOutput, calls=%fused_computation.123 | convolution fusion | flops 6442450944 | bytes 11534336 | tf_op jit(solution)/shard_map/dot_general | solution.py:17
  18.0 80.7 %all-reduce.9.cloned.1.call-done = f32[1024,256]{1,0:T(8,128)} async-done(((f32[1024,256]{1,0:T(8,128)}), f32[1024,256]{1,0:T(8,128)}) %all-reduce.9.cloned.1.call-update) | async-done | bytes 1048592 | tf_op jit(solution)/shard_map/psum | solution.py:28
  98.6 4.1 convolution_multiply_fusion.1
  102.8 10.7 %fusion.51 = f32[256,2048]{1,0:T(8,128)} fusion(f32[256,1024]{1,0:T(8,128)S(1)} %copy-done.12, f32[1024,2048]{1,0:T(8,128)} %param.6), kind=kOutput, calls=%fused_computation.124 | convolution fusion | flops 6442450944 | bytes 11534336 | tf_op jit(solution)/shard_map/dot_general | solution.py:17
  113.5 127.4 %all-reduce.11.cloned.1.call-done = f32[256,256]{0,1:T(8,128)} async-done(((f32[256,256]{0,1:T(8,128)}), f32[256,256]{0,1:T(8,128)}) %all-reduce.11.cloned.1.call-update) | async-done | bytes 262160 | tf_op jit(solution)/shard_map/psum | solution.py:30
  243.7 11.7 %cholesky.214 = f32[128,128]{1,0:T(8,128)S(1)} custom-call(f32[128,128]{1,0:T(8,128)S(1)} %cholesky.346), custom_call_target="Cholesky" | custom-call | tf_op jit(solution)/shard_map/jit(cholesky)/cholesky | solution.py:32
  255.5 9.8 %custom-call.37 = f32[1,128,128]{1,2,0:T(8,128)S(1)} custom-call(f32[1,128,128]{2,1,0:T(8,128)S(1)} %get-tuple-element.96), custom_call_target="InvertDiagBlocksLowerTriangular" | custom-call | tf_op jit(solution)/shard_map/jit(cholesky)/cholesky | solution.py:32
  267.4 11.7 %cholesky.231 = f32[128,128]{1,0:T(8,128)S(1)} custom-call(f32[128,128]{1,0:T(8,128)S(1)} %convolution_subtract_fusion.9), custom_call_target="Cholesky" | custom-call | tf_op jit(solution)/shard_map/jit(cholesky)/cholesky | solution.py:32
  282.3 4.1 while.4
  282.9 1.4 bitcast_dynamic-update-slice_fusion.8
  284.9 1.4 bitcast_dynamic-update-slice_fusion.8
  287.0 20.7 %custom-call.30 = f32[2,128,128]{1,2,0:T(8,128)S(1)} custom-call(f32[2,128,128]{2,1,0:T(8,128)} %copy-done.17), custom_call_target="InvertDiagBlocksLowerTriangular" | custom-call | tf_op jit(solution)/shard_map/jit(_solve_triangular)/triangular_solve | solution.py:34
  310.0 2.8 convolution_bitcast_fusion
  312.9 16.9 %fusion.54 = f32[512,2048]{1,0:T(8,128)S(1)} fusion(f32[512,1024]{1,0:T(8,128)S(1)} %copy-done, f32[1024,2048]{1,0:T(8,128)} %param.6), kind=kOutput, calls=%fused_computation.127 | convolution fusion | flops 12884901888 | bytes 14680064 | tf_op jit(solution)/shard_map/dot_general | solution.py:17
  329.8 7.9 fusion.55
  337.7 2.8 all-reduce.13.cloned.1.call-start
  341.6 2.5 copy.14
  344.1 116.8 %all-reduce.19.cloned.1.call-done = (f32[256,2048]{1,0:T(8,128)}, f32[512,256]{0,1:T(8,128)}) async-done(((f32[256,2048]{1,0:T(8,128)}, f32[512,256]{0,1:T(8,128)}), (f32[256,2048]{1,0:T(8,128)}, f32[512,256]{0,1:T(8,128)})) %all-reduce.19.cloned.1.call-update) | async-done | bytes 2621456 | tf_op jit(solution)/shard_map/psum | solution.py:29
  460.9 1.8 fusion.53
  462.9 11.7 %cholesky.316 = f32[128,128]{1,0:T(8,128)S(1)} custom-call(f32[128,128]{1,0:T(8,128)S(1)} %cholesky.355), custom_call_target="Cholesky" | custom-call | tf_op jit(solution)/shard_map/jit(cholesky)/cholesky | solution.py:41
  474.7 9.8 %custom-call.40 = f32[1,128,128]{1,2,0:T(8,128)S(1)} custom-call(f32[1,128,128]{2,1,0:T(8,128)S(1)} %get-tuple-element.88), custom_call_target="InvertDiagBlocksLowerTriangular" | custom-call | tf_op jit(solution)/shard_map/jit(cholesky)/cholesky | solution.py:41
  485.0 11.7 %cholesky.333 = f32[128,128]{1,0:T(8,128)S(1)} custom-call(f32[128,128]{1,0:T(8,128)S(1)} %convolution_subtract_fusion.6), custom_call_target="Cholesky" | custom-call | tf_op jit(solution)/shard_map/jit(cholesky)/cholesky | solution.py:41
  499.5 4.1 while.7
  500.1 1.4 bitcast_dynamic-update-slice_fusion.11
  502.2 1.4 bitcast_dynamic-update-slice_fusion.11
  503.6 19.7 %custom-call.33 = f32[2,128,128]{1,2,0:T(8,128)S(1)} custom-call(f32[2,128,128]{2,1,0:T(8,128)S(1)} %get-tuple-element.35), custom_call_target="InvertDiagBlocksLowerTriangular" | custom-call | tf_op jit(solution)/shard_map/jit(_cho_solve)/triangular_solve | solution.py:41
  523.3 4.8 convolution_multiply_fusion
  528.6 85.9 %all-reduce.17.cloned.1.call-done = f32[512,512]{1,0:T(8,128)} async-done(((f32[512,512]{1,0:T(8,128)}), f32[512,512]{1,0:T(8,128)}) %all-reduce.17.cloned.1.call-update) | async-done | bytes 1048592 | tf_op jit(solution)/shard_map/psum | solution.py:27
  614.5 2.3 fusion.56
  618.1 73.0 %all-reduce.13.cloned.1.call-done = f32[256,256]{0,1:T(8,128)} async-done(((f32[256,256]{0,1:T(8,128)}), f32[256,256]{0,1:T(8,128)}) %all-reduce.13.cloned.1.call-update) | async-done | bytes 262160 | tf_op jit(solution)/shard_map/psum | solution.py:31
  693.2 11.7 %cholesky.248 = f32[128,128]{1,0:T(8,128)S(1)} custom-call(f32[128,128]{1,0:T(8,128)S(1)} %cholesky.349), custom_call_target="Cholesky" | custom-call | tf_op jit(solution)/shard_map/jit(cholesky)/cholesky | solution.py:33
  705.0 9.8 %custom-call.38 = f32[1,128,128]{1,2,0:T(8,128)S(1)} custom-call(f32[1,128,128]{2,1,0:T(8,128)S(1)} %get-tuple-element.92), custom_call_target="InvertDiagBlocksLowerTriangular" | custom-call | tf_op jit(solution)/shard_map/jit(cholesky)/cholesky | solution.py:33
  716.9 11.9 %cholesky.265 = f32[128,128]{1,0:T(8,128)S(1)} custom-call(f32[128,128]{1,0:T(8,128)S(1)} %convolution_subtract_fusion.8), custom_call_target="Cholesky" | custom-call | tf_op jit(solution)/shard_map/jit(cholesky)/cholesky | solution.py:33
  731.5 4.0 while.5
  734.1 1.4 bitcast_dynamic-update-slice_fusion.9
  735.5 19.7 %custom-call.31 = f32[2,128,128]{1,2,0:T(8,128)S(1)} custom-call(f32[2,128,128]{2,1,0:T(8,128)S(1)} %get-tuple-element.19), custom_call_target="InvertDiagBlocksLowerTriangular" | custom-call | tf_op jit(solution)/shard_map/jit(_solve_triangular)/triangular_solve | solution.py:35
  755.2 2.4 fusion
  761.2 1.4 copy-done.3
  762.6 4.5 convolution_bitcast_fusion.1
  768.3 73.2 %all-reduce.15.cloned.1.call-done = f32[512,256]{0,1:T(8,128)} async-done(((f32[512,256]{0,1:T(8,128)}), f32[512,256]{0,1:T(8,128)}) %all-reduce.15.cloned.1.call-update) | async-done | bytes 524304 | tf_op jit(solution)/shard_map/psum | solution.py:37
  841.5 1.8 fusion.52
  845.9 11.9 %cholesky.282 = f32[128,128]{1,0:T(8,128)S(1)} custom-call(f32[128,128]{1,0:T(8,128)S(1)} %cholesky.352), custom_call_target="Cholesky" | custom-call | tf_op jit(solution)/shard_map/jit(cholesky)/cholesky | solution.py:43
  857.8 9.8 %custom-call.39 = f32[1,128,128]{1,2,0:T(8,128)S(1)} custom-call(f32[1,128,128]{2,1,0:T(8,128)S(1)} %get-tuple-element.84), custom_call_target="InvertDiagBlocksLowerTriangular" | custom-call | tf_op jit(solution)/shard_map/jit(cholesky)/cholesky | solution.py:43
  869.8 11.7 %cholesky.299 = f32[128,128]{1,0:T(8,128)S(1)} custom-call(f32[128,128]{1,0:T(8,128)S(1)} %convolution_subtract_fusion.7), custom_call_target="Cholesky" | custom-call | tf_op jit(solution)/shard_map/jit(cholesky)/cholesky | solution.py:43
  885.2 4.1 while.6
  885.8 1.4 bitcast_dynamic-update-slice_fusion.10
  887.9 1.4 bitcast_dynamic-update-slice_fusion.10
  890.0 20.5 %custom-call.32 = f32[2,128,128]{1,2,0:T(8,128)S(1)} custom-call(f32[2,128,128]{2,1,0:T(8,128)} %copy-done.16), custom_call_target="InvertDiagBlocksLowerTriangular" | custom-call | tf_op jit(solution)/shard_map/jit(_cho_solve)/triangular_solve | solution.py:43
  (134 shorter events, 42.4 us)
Async XLA Ops:
  7.2 302.9 %copy-start = (f32[512,1024]{1,0:T(8,128)S(1)}, f32[512,1024]{1,0:T(8,128)}, u32[]{:S(2)}) copy-start(f32[512,1024]{1,0:T(8,128)} %param.9) | copy-start | bytes 6291460
  7.2 91.5 %all-reduce.9.cloned.1.call-start = ((), (), s32[]{:S(2)}) async-start(), calls=%async_computation | async-start | bytes 2097152 | tf_op jit(solution)/shard_map/psum | solution.py:28
  17.9 84.9 %copy-start.12 = (f32[256,1024]{1,0:T(8,128)S(1)}, f32[256,1024]{1,0:T(8,128)}, u32[]{:S(2)}) copy-start(f32[256,1024]{1,0:T(8,128)} %param.8) | copy-start | bytes 3145732
  17.9 223.0 %all-reduce.11.cloned.1.call-start = ((), (), s32[]{:S(2)}) async-start(), calls=%async_computation.1 | async-start | bytes 524288 | tf_op jit(solution)/shard_map/psum | solution.py:30
  102.7 358.2 %all-reduce.19.cloned.1.call-start = ((), (), s32[]{:S(2)}) async-start(), calls=%async_computation.5 | async-start | bytes 5242880 | tf_op jit(solution)/shard_map/psum | solution.py:29
  113.5 194.2 %copy-start.4 = (f32[1024,256]{1,0:T(8,128)S(1)}, f32[1024,256]{1,0:T(8,128)}, u32[]{:S(2)}) copy-start(f32[1024,256]{1,0:T(8,128)} %all-reduce.9.cloned.1.call-done) | copy-start | bytes 3145732
  243.0 0.7 copy-start.13
  279.2 2.0 copy-start.10
  286.4 0.7 copy-start.17
  308.4 1.7 copy-start.5
  312.8 301.7 %all-reduce.17.cloned.1.call-start = ((), (), s32[]{:S(2)}) async-start(), calls=%async_computation.4 | async-start | bytes 2097152 | tf_op jit(solution)/shard_map/psum | solution.py:27
  312.9 16.9 %copy-start.2 = (f32[512,2048]{1,0:T(8,128)S(1)}, f32[512,2048]{1,0:T(8,128)}, u32[]{:S(2)}) copy-start(f32[512,2048]{1,0:T(8,128)} %param.10) | copy-start | bytes 12582916
  329.8 10.7 %copy-start.6 = (f32[128,1024]{1,0:T(8,128)S(1)}, f32[128,1024]{1,0:T(8,128)}, u32[]{:S(2)}) copy-start(f32[128,1024]{1,0:T(8,128)} %copy-done.5) | copy-start | bytes 1572868
  337.7 353.3 %all-reduce.13.cloned.1.call-start = ((), (), s32[]{:S(2)}) async-start(), calls=%async_computation.2 | async-start | bytes 524288 | tf_op jit(solution)/shard_map/psum | solution.py:31
  523.3 91.3 %copy-start.9 = (f32[512,256]{0,1:T(8,128)S(1)}, f32[512,256]{0,1:T(8,128)}, u32[]{:S(2)}) copy-start(f32[512,256]{0,1:T(8,128)} %get-tuple-element.72) | copy-start | bytes 1572868
  528.2 313.4 %all-reduce.15.cloned.1.call-start = ((), (), s32[]{:S(2)}) async-start(), calls=%async_computation.3 | async-start | bytes 1048576 | tf_op jit(solution)/shard_map/psum | solution.py:37
  693.2 11.7 %copy-start.14 = (f32[256,256]{1,0:T(8,128)}, f32[256,256]{1,0:T(8,128)S(1)}, u32[]{:S(2)}) copy-start(f32[256,256]{1,0:T(8,128)S(1)} %fusion.14) | copy-start | bytes 786436
  755.2 2.4 copy-start.1
  759.7 2.9 copy-start.3
  759.9 1.3 copy-start.7
  843.3 67.1 %copy-start.8 = (f32[512,256]{0,1:T(8,128)S(1)}, f32[512,256]{0,1:T(8,128)}, u32[]{:S(2)}) copy-start(f32[512,256]{0,1:T(8,128)} %all-reduce.15.cloned.1.call-done) | copy-start | bytes 1572868
  845.2 0.7 copy-start.15
  882.3 1.9 copy-start.11
  889.3 0.7 copy-start.16
Sparse Core Ops, SparseCore 0:
  18.1 80.5 all-reduce.8
  102.8 138.0 all-reduce.10
  313.0 147.9 all-reduce.18
  465.6 148.9 all-reduce.16
  617.4 73.6 all-reduce.12
  767.3 74.1 all-reduce.14
where the time goes:
time: 929 us; the launch traced here: 921 us
  waiting for transfers between devices  557 us (60%)
  other arithmetic  225 us (24%)
  matrix products  86.6 us (9%)
  local copies, waits for them, and re-layouts  28.3 us (3%)
  between operations  20.2 us (2%)
    psum x1, waiting for transfers between devices, per_device(): gram_y = lax.psum(inner_rows(range_full, range_full) / rows_total, 'cell')  127 us
    psum x1, waiting for transfers between devices, per_device(): co_full = lax.psum(co_term, 'cell')  117 us
    psum x1, waiting for transfers between devices, per_device(): sketch_z = lax.psum(core_term, ('cell', 'tm'))  85.9 us
    psum x1, waiting for transfers between devices, per_device(): range_full = lax.psum(range_term, 'tm')  80.7 us
    psum x1, waiting for transfers between devices, per_device(): right_image = lax.psum(inner_cols(core_right, co_basis), 'tm')  73.2 us
    psum x1, waiting for transfers between devices, per_device(): gram_w = lax.psum(inner_cols(co_full, co_full) / cols_total, 'tm')  73 us
    dot_general x5, matrix products, product(): jnp.dot(left, right, precision=lax.Precision.HIGHEST, preferred_element_t...  41.6 us
    another operation x7, other arithmetic, per_device(): jnp.linalg.cholesky(gram_right)  34.8 us
  transfers between devices with their start and end apart: 6, of which 6 were waited for; matrix products, arithmetic and copies ran while one was open for 12% of the time, Pallas kernels for 0%

commit v1 on v0

--- a/solution.py
+++ b/solution.py
@@ -25,7 +25,7 @@
     left_window = product(core_left, window)
     core_term = inner_cols(left_window, core_right)
     sketch_z = lax.psum(core_term, ("cell", "tm"))
-    range_full = lax.psum(range_term, "tm")
+    range_full = jnp.sum(lax.all_gather(range_term, "tm"), axis=0)
     co_full = lax.psum(co_term, "cell")
     gram_y = lax.psum(inner_rows(range_full, range_full) / rows_total, "cell")
     gram_w = lax.psum(inner_cols(co_full, co_full) / cols_total, "tm")

time: 929 us -> 1030 us (1.11)
  waiting for transfers between devices: 557 us -> 651 us
    all_gather x0 -> x1, waiting for transfers between devices: none -> 171 us  [per_device(): range_full = jnp.sum(lax.all_gather(range_term, 'tm'), axis=0)]
    psum x1 -> x0, waiting for transfers between devices: 80.7 us -> none  [per_device(): range_full = lax.psum(range_term, 'tm')]
  transfers between devices with their start and end apart: 6 -> 6, of which waited for: 6 -> 6; matrix products, arithmetic and copies ran while one was open for 12% -> 11% of each run, Pallas kernels for 0% -> 0%
where the time goes in v1:
time: 1030 us; the launch traced here: 1020 us
  waiting for transfers between devices  651 us (63%)
  other arithmetic  229 us (22%)
  matrix products  85.4 us (8%)
  local copies, waits for them, and re-layouts  28.3 us (3%)
  between operations  20.2 us (2%)
    all_gather x1, waiting for transfers between devices, per_device(): range_full = jnp.sum(lax.all_gather(range_term, 'tm'), axis=0)  171 us
    psum x1, waiting for transfers between devices, per_device(): gram_y = lax.psum(inner_rows(range_full, range_full) / rows_total, 'cell')  130 us
    psum x1, waiting for transfers between devices, per_device(): co_full = lax.psum(co_term, 'cell')  117 us
    psum x1, waiting for transfers between devices, per_device(): sketch_z = lax.psum(core_term, ('cell', 'tm'))  85.8 us
    psum x1, waiting for transfers between devices, per_device(): right_image = lax.psum(inner_cols(core_right, co_basis), 'tm')  73.5 us
    psum x1, waiting for transfers between devices, per_device(): gram_w = lax.psum(inner_cols(co_full, co_full) / cols_total, 'tm')  73 us
    dot_general x5, matrix products, product(): jnp.dot(left, right, precision=lax.Precision.HIGHEST, preferred_element_t...  41.9 us
    another operation x7, other arithmetic, per_device(): jnp.linalg.cholesky(gram_right)  34.8 us
  transfers between devices with their start and end apart: 6, of which 6 were waited for; matrix products, arithmetic and copies ran while one was open for 11% of the time, Pallas kernels for 0%

profile of v1, /device:TPU:0, one launch (start us, length us, event | category | flops | bytes accessed | tf_op | source)
XLA Modules:
  0.0 1017.1 jit_solution(13753096916916904676)
XLA Ops:
  7.2 10.7 %fusion.50 = f32[1024,256]{1,0:T(8,128)} fusion(f32[1024,2048]{1,0:T(8,128)} %param.6, f32[2048,256]{1,0:T(8,128)} %param.7), kind=kOutput, calls=%fused_computation.123 | convolution fusion | flops 6442450944 | bytes 11534336 | tf_op jit(solution)/shard_map/dot_general | solution.py:17
  18.0 171.0 %all-gather.3.cloned.1.call-done = f32[8192,256]{1,0:T(8,128)} async-done(((f32[1024,256]{1,0:T(8,128)}), f32[8192,256]{1,0:T(8,128)}) %all-gather.3.cloned.1.call-update) | async-done | bytes 8388624 | tf_op jit(solution)/shard_map/all_gather | solution.py:28
  188.9 4.1 reduce_sum.9
  193.0 2.5 convolution_multiply_fusion.1
  195.6 11.0 %fusion.51 = f32[256,2048]{1,0:T(8,128)} fusion(f32[256,1024]{1,0:T(8,128)} %param.8, f32[1024,2048]{1,0:T(8,128)} %param.6), kind=kOutput, calls=%fused_computation.124 | convolution fusion | flops 6442450944 | bytes 11534336 | tf_op jit(solution)/shard_map/dot_general | solution.py:17
  206.6 130.5 %all-reduce.8.cloned.1.call-done = f32[256,256]{0,1:T(8,128)} async-done(((f32[256,256]{0,1:T(8,128)}), f32[256,256]{0,1:T(8,128)}) %all-reduce.8.cloned.1.call-update) | async-done | bytes 262160 | tf_op jit(solution)/shard_map/psum | solution.py:30
  339.9 11.7 %cholesky.214 = f32[128,128]{1,0:T(8,128)S(1)} custom-call(f32[128,128]{1,0:T(8,128)S(1)} %cholesky.346), custom_call_target="Cholesky" | custom-call | tf_op jit(solution)/shard_map/jit(cholesky)/cholesky | solution.py:32
  351.6 9.8 custom-call.37
  363.6 11.7 %cholesky.231 = f32[128,128]{1,0:T(8,128)S(1)} custom-call(f32[128,128]{1,0:T(8,128)S(1)} %convolution_subtract_fusion.9), custom_call_target="Cholesky" | custom-call | tf_op jit(solution)/shard_map/jit(cholesky)/cholesky | solution.py:32
  378.4 4.1 while.4
  379.1 1.4 bitcast_dynamic-update-slice_fusion.8
  381.1 1.4 bitcast_dynamic-update-slice_fusion.8
  383.2 20.7 %custom-call.30 = f32[2,128,128]{1,2,0:T(8,128)S(1)} custom-call(f32[2,128,128]{2,1,0:T(8,128)} %copy-done.15), custom_call_target="InvertDiagBlocksLowerTriangular" | custom-call | tf_op jit(solution)/shard_map/jit(_solve_triangular)/triangular_solve | solution.py:34
  406.2 2.8 convolution_bitcast_fusion
  409.1 16.9 %fusion.54 = f32[512,2048]{1,0:T(8,128)S(1)} fusion(f32[512,1024]{1,0:T(8,128)S(1)} %copy-done, f32[1024,2048]{1,0:T(8,128)} %param.6), kind=kOutput, calls=%fused_computation.127 | convolution fusion | flops 12884901888 | bytes 14680064 | tf_op jit(solution)/shard_map/dot_general | solution.py:17
  426.0 7.9 fusion.55
  433.9 2.8 all-reduce.10.cloned.1.call-start
  437.7 2.5 copy.14
  440.3 116.8 %all-reduce.16.cloned.1.call-done = (f32[256,2048]{1,0:T(8,128)}, f32[512,256]{0,1:T(8,128)}) async-done(((f32[256,2048]{1,0:T(8,128)}, f32[512,256]{0,1:T(8,128)}), (f32[256,2048]{1,0:T(8,128)}, f32[512,256]{0,1:T(8,128)})) %all-reduce.16.cloned.1.call-update) | async-done | bytes 2621456 | tf_op jit(solution)/shard_map/psum | solution.py:29
  557.1 1.8 fusion.53
  559.1 11.7 %cholesky.316 = f32[128,128]{1,0:T(8,128)S(1)} custom-call(f32[128,128]{1,0:T(8,128)S(1)} %cholesky.355), custom_call_target="Cholesky" | custom-call | tf_op jit(solution)/shard_map/jit(cholesky)/cholesky | solution.py:41
  570.9 9.8 custom-call.40
  581.2 11.7 %cholesky.333 = f32[128,128]{1,0:T(8,128)S(1)} custom-call(f32[128,128]{1,0:T(8,128)S(1)} %convolution_subtract_fusion.6), custom_call_target="Cholesky" | custom-call | tf_op jit(solution)/shard_map/jit(cholesky)/cholesky | solution.py:41
  595.7 4.1 while.7
  596.3 1.4 bitcast_dynamic-update-slice_fusion.11
  598.3 1.4 bitcast_dynamic-update-slice_fusion.11
  599.8 19.7 %custom-call.33 = f32[2,128,128]{1,2,0:T(8,128)S(1)} custom-call(f32[2,128,128]{2,1,0:T(8,128)S(1)} %get-tuple-element.35), custom_call_target="InvertDiagBlocksLowerTriangular" | custom-call | tf_op jit(solution)/shard_map/jit(_cho_solve)/triangular_solve | solution.py:41
  619.5 4.8 convolution_multiply_fusion
  624.8 85.8 %all-reduce.14.cloned.1.call-done = f32[512,512]{1,0:T(8,128)} async-done(((f32[512,512]{1,0:T(8,128)}), f32[512,512]{1,0:T(8,128)}) %all-reduce.14.cloned.1.call-update) | async-done | bytes 1048592 | tf_op jit(solution)/shard_map/psum | solution.py:27
  710.5 2.3 fusion.56
  714.0 73.0 %all-reduce.10.cloned.1.call-done = f32[256,256]{0,1:T(8,128)} async-done(((f32[256,256]{0,1:T(8,128)}), f32[256,256]{0,1:T(8,128)}) %all-reduce.10.cloned.1.call-update) | async-done | bytes 262160 | tf_op jit(solution)/shard_map/psum | solution.py:31
  789.2 11.7 %cholesky.248 = f32[128,128]{1,0:T(8,128)S(1)} custom-call(f32[128,128]{1,0:T(8,128)S(1)} %cholesky.349), custom_call_target="Cholesky" | custom-call | tf_op jit(solution)/shard_map/jit(cholesky)/cholesky | solution.py:33
  801.0 9.8 custom-call.38
  812.9 11.9 %cholesky.265 = f32[128,128]{1,0:T(8,128)S(1)} custom-call(f32[128,128]{1,0:T(8,128)S(1)} %convolution_subtract_fusion.8), custom_call_target="Cholesky" | custom-call | tf_op jit(solution)/shard_map/jit(cholesky)/cholesky | solution.py:33
  827.5 4.0 while.5
  831.5 19.7 %custom-call.31 = f32[2,128,128]{1,2,0:T(8,128)S(1)} custom-call(f32[2,128,128]{2,1,0:T(8,128)S(1)} %get-tuple-element.19), custom_call_target="InvertDiagBlocksLowerTriangular" | custom-call | tf_op jit(solution)/shard_map/jit(_solve_triangular)/triangular_solve | solution.py:35
  851.2 2.4 fusion
  857.2 1.4 copy-done.3
  858.6 4.5 convolution_bitcast_fusion.1
  864.3 73.5 %all-reduce.12.cloned.1.call-done = f32[512,256]{0,1:T(8,128)} async-done(((f32[512,256]{0,1:T(8,128)}), f32[512,256]{0,1:T(8,128)}) %all-reduce.12.cloned.1.call-update) | async-done | bytes 524304 | tf_op jit(solution)/shard_map/psum | solution.py:37
  937.8 1.8 fusion.52
  942.2 11.9 %cholesky.282 = f32[128,128]{1,0:T(8,128)S(1)} custom-call(f32[128,128]{1,0:T(8,128)S(1)} %cholesky.352), custom_call_target="Cholesky" | custom-call | tf_op jit(solution)/shard_map/jit(cholesky)/cholesky | solution.py:43
  954.1 9.8 custom-call.39
  966.1 11.7 %cholesky.299 = f32[128,128]{1,0:T(8,128)S(1)} custom-call(f32[128,128]{1,0:T(8,128)S(1)} %convolution_subtract_fusion.7), custom_call_target="Cholesky" | custom-call | tf_op jit(solution)/shard_map/jit(cholesky)/cholesky | solution.py:43
  981.5 4.1 while.6
  982.1 1.4 bitcast_dynamic-update-slice_fusion.10
  984.1 1.4 bitcast_dynamic-update-slice_fusion.10
  986.2 20.5 %custom-call.32 = f32[2,128,128]{1,2,0:T(8,128)S(1)} custom-call(f32[2,128,128]{2,1,0:T(8,128)} %copy-done.14), custom_call_target="InvertDiagBlocksLowerTriangular" | custom-call | tf_op jit(solution)/shard_map/jit(_cho_solve)/triangular_solve | solution.py:43
  (131 shorter events, 43.8 us)
Async XLA Ops:
  7.2 399.0 %copy-start = (f32[512,1024]{1,0:T(8,128)S(1)}, f32[512,1024]{1,0:T(8,128)}, u32[]{:S(2)}) copy-start(f32[512,1024]{1,0:T(8,128)} %param.9) | copy-start | bytes 6291460
  7.2 181.8 %all-gather.3.cloned.1.call-start = ((), (), s32[]{:S(2)}) async-start(), calls=%async_computation.4 | async-start | bytes 9437184 | tf_op jit(solution)/shard_map/all_gather | solution.py:28
  17.9 319.2 %all-reduce.8.cloned.1.call-start = ((), (), s32[]{:S(2)}) async-start(), calls=%async_computation | async-start | bytes 524288 | tf_op jit(solution)/shard_map/psum | solution.py:30
  195.6 361.5 %all-reduce.16.cloned.1.call-start = ((), (), s32[]{:S(2)}) async-start(), calls=%async_computation.5 | async-start | bytes 5242880 | tf_op jit(solution)/shard_map/psum | solution.py:29
  339.2 0.7 copy-start.11
  375.4 2.0 copy-start.9
  382.5 0.7 copy-start.15
  404.5 1.7 copy-start.4
  409.0 301.5 %all-reduce.14.cloned.1.call-start = ((), (), s32[]{:S(2)}) async-start(), calls=%async_computation.3 | async-start | bytes 2097152 | tf_op jit(solution)/shard_map/psum | solution.py:27
  409.0 16.9 %copy-start.2 = (f32[512,2048]{1,0:T(8,128)S(1)}, f32[512,2048]{1,0:T(8,128)}, u32[]{:S(2)}) copy-start(f32[512,2048]{1,0:T(8,128)} %param.10) | copy-start | bytes 12582916
  426.0 10.7 %copy-start.5 = (f32[128,1024]{1,0:T(8,128)S(1)}, f32[128,1024]{1,0:T(8,128)}, u32[]{:S(2)}) copy-start(f32[128,1024]{1,0:T(8,128)} %copy-done.4) | copy-start | bytes 1572868
  433.9 353.2 %all-reduce.10.cloned.1.call-start = ((), (), s32[]{:S(2)}) async-start(), calls=%async_computation.1 | async-start | bytes 524288 | tf_op jit(solution)/shard_map/psum | solution.py:31
  619.4 91.1 %copy-start.8 = (f32[512,256]{0,1:T(8,128)S(1)}, f32[512,256]{0,1:T(8,128)}, u32[]{:S(2)}) copy-start(f32[512,256]{0,1:T(8,128)} %get-tuple-element.72) | copy-start | bytes 1572868
  624.3 313.5 %all-reduce.12.cloned.1.call-start = ((), (), s32[]{:S(2)}) async-start(), calls=%async_computation.2 | async-start | bytes 1048576 | tf_op jit(solution)/shard_map/psum | solution.py:37
  789.1 11.7 %copy-start.12 = (f32[256,256]{1,0:T(8,128)}, f32[256,256]{1,0:T(8,128)S(1)}, u32[]{:S(2)}) copy-start(f32[256,256]{1,0:T(8,128)S(1)} %fusion.14) | copy-start | bytes 786436
  851.2 2.4 copy-start.1
  855.7 2.9 copy-start.3
  855.9 1.3 copy-start.6
  939.6 67.1 %copy-start.7 = (f32[512,256]{0,1:T(8,128)S(1)}, f32[512,256]{0,1:T(8,128)}, u32[]{:S(2)}) copy-start(f32[512,256]{0,1:T(8,128)} %all-reduce.12.cloned.1.call-done) | copy-start | bytes 1572868
  941.4 0.7 copy-start.13
  978.6 1.9 copy-start.10
  985.6 0.7 copy-start.14
Sparse Core Ops, SparseCore 0:
  18.1 170.8 all-gather.2
  195.7 141.3 all-reduce.7
  409.1 147.9 all-reduce.15
  561.7 148.7 all-reduce.13
  713.4 73.6 all-reduce.9
  863.3 74.4 all-reduce.11
